TPU v7x, 32 devices: a whole 2x2x4 slice. The times are simulated.
32 devices in a mesh: groups: 2 (over y), block: 4 (over x, core), tensor: 4 (over z).
Axes of the slice: x: 2, y: 2, z: 4, core: 2. Of those that a mesh axis runs over, the one named last changes fastest.
Arguments:
- tokens: bfloat16 [4096, 5120], P(('groups', 'block', 'tensor')), parts along dimension 0, may hold values from -20 to 20
- mod_shift: float32 [5120], replicated, may hold values from -3 to 3
- mod_scale: float32 [5120], replicated, may hold values from -0.5 to 0.5
- w_qkv: bfloat16 [3, 5120, 1024], P(None, 'block', 'tensor'), may hold values from -1 to 1
- tile_list: int32 [8, 4, 5], P(('groups', 'block')), parts along dimension 0, may hold values from 0 to 7, as said below
- tile_count: int32 [8, 4], P(('groups', 'block')), parts along dimension 0, may hold values from 2 to 5, as said below
Outputs:
- attended: bfloat16 [4096, 1024], P(('groups', 'block'), 'tensor'), parts along dimension 0
There are 2 independent parts, one for each index of `groups`. A program takes and returns all parts, laid end to end along the dimension named above; an argument that names none is the same for every part. Nothing has to cross between parts.
Inputs may be any that keep to these rules, and one draw needn't show every extreme that they name: `tile_list`: within the first tile_count[c, t] slots the entries are distinct, the first is the query tile itself (2 + t), and none names a tile outside the slab; blocks at scene cuts name no tile of the block across the cut. Later slots hold indices in range and are not read. `tile_count`: the first query tile of every block reads 5 slots.
All inputs are finite; a program needn't handle non-finite values.
Results may differ from a plain program's by a relative error of at most 0.0087.
Values may be sent and summed in bfloat16 or wider, within the bound.
No kernel may reach another device: no remote copies, remote signals or barrier semaphores. Data moves between devices by JAX's collectives and lax.ppermute only.
A program may use at most 64 MiB of HBM per device.

v0:
```python
import jax
import jax.numpy as jnp
from jax import lax
from jax.sharding import PartitionSpec as P

HEAD_DIM = 128
TILE = 128
BT = 2
epsilon = 1e-06


def with_halo(x, sides, width):
    for axis, dim in sides:
        count, length = (lax.axis_size(axis), x.shape[dim])
        up = [(i, (i + 1) % count) for i in range(count - 1)]
        down = [(j, i) for i, j in up]
        last = lax.slice_in_dim(x, length - width, length, axis=dim)
        first = lax.slice_in_dim(x, 0, width, axis=dim)
        before = lax.ppermute(last, axis, up)
        after = lax.ppermute(first, axis, down)
        x = jnp.concatenate([before, x, after], axis=dim)
    return x


def attend(queries, key_rows, value_rows, chosen_list, chosen_count):
    head_count = queries.shape[1] // HEAD_DIM
    local_tiles = queries.shape[0] // TILE
    all_tiles = key_rows.shape[0] // TILE
    slot_count = chosen_list.shape[1]
    shaped_queries = queries.reshape(local_tiles, TILE, head_count, HEAD_DIM)
    key_tiles = key_rows.reshape(all_tiles, TILE, head_count, HEAD_DIM)[chosen_list]
    value_tiles = value_rows.reshape(all_tiles, TILE, head_count, HEAD_DIM)[chosen_list]
    scores = jnp.einsum(
        "pthd,pkshd->phtks", shaped_queries, key_tiles, preferred_element_type=jnp.float32
    )
    scores = scores * HEAD_DIM ** (-0.5)
    live_slot = jnp.arange(slot_count, dtype=jnp.int32)[None, :] < chosen_count[:, None]
    scores = jnp.where(live_slot[:, None, None, :, None], scores, jnp.float32(-1e30))
    highest = jnp.max(scores, axis=(3, 4), keepdims=True)
    exponent = jnp.exp(scores - highest)
    denominator = jnp.sum(exponent, axis=(3, 4), keepdims=True)
    attn_weights = (exponent / denominator).astype(jnp.bfloat16)
    mixed = jnp.einsum(
        "phtks,pkshd->pthd", attn_weights, value_tiles, preferred_element_type=jnp.float32
    )
    return mixed.astype(jnp.bfloat16).reshape(local_tiles * TILE, head_count * HEAD_DIM)


def shards(tokens, mod_shift, mod_scale, w_qkv, tile_list, tile_count):
    values_in = tokens.astype(jnp.float32)
    row_mean = jnp.mean(values_in, axis=1, keepdims=True)
    centred = values_in - row_mean
    row_var = jnp.mean(centred * centred, axis=1, keepdims=True)
    normed = (centred * lax.rsqrt(row_var + epsilon) * (1.0 + mod_scale) + mod_shift).astype(
        jnp.bfloat16
    )
    gathered = lax.all_gather(normed, "tensor", axis=0, tiled=True)
    projected = jnp.einsum(
        "td,ide->ite",
        gathered,
        lax.all_gather(w_qkv, "block", axis=1, tiled=True),
        preferred_element_type=jnp.float32,
    )
    projected = projected.astype(jnp.bfloat16)
    queries = projected[0]
    key_value = projected[1:3]
    extended = with_halo(key_value, (("block", 1),), BT * TILE)
    return attend(queries, extended[0], extended[1], tile_list[0], tile_count[0])


def solution(mesh):
    return jax.shard_map(
        shards,
        mesh=mesh,
        in_specs=(
            P(("groups", "block", "tensor"), None),
            P(),
            P(),
            P(None, "block", "tensor"),
            P(("groups", "block"), None, None),
            P(("groups", "block"), None),
        ),
        out_specs=P(("groups", "block"), "tensor"),
        check_vma=False,
    )
```

profile of v0, /device:TPU:1, one launch (start us, length us, event | category | flops | bytes accessed | tf_op | source)
XLA Modules:
  0.0 203.5 jit_solution(6897856617463823574)
XLA Ops:
  6.5 0.0 copy-start
  6.5 0.0 copy-start.2
  6.5 0.0 copy-start.1
  6.5 0.0 all-gather.3.cloned.1.call-start
  6.5 1.7 convert_reduce_fusion
  8.2 1.8 fusion.4
  10.1 0.0 copy-done.2
  10.1 0.0 copy-done
  10.1 0.0 copy-done.1
  10.1 0.0 copy-start.3
  10.1 1.7 fusion.7
  11.8 0.0 all-gather.3.cloned.1.call-update
  11.8 0.0 all-gather.5.cloned.1.call-start
  11.9 0.7 all-gather.5.cloned.1.call-update
  12.6 0.0 copy-done.3
  12.6 0.1 reshape.73
  12.7 0.0 copy-start.4
  12.7 99.4 %all-gather.3.cloned.1.call-done = bf16[512,5120]{1,0:T(8,128)(2,1)} async-done(((bf16[128,5120]{1,0:T(8,128)(2,1)}), bf16[512,5120]{1,0:T(8,128)(2,1)}) %all-gather.3.cloned.1.call-update) | async-done | bytes 5242896 | tf_op jit(solution)/shard_map/all_gather | solution.py:57
  112.1 55.6 %all-gather.5.cloned.1.call-done = bf16[3,5120,256]{2,1,0:T(8,128)(2,1)} async-done(((bf16[3,1280,256]{2,1,0:T(8,128)(2,1)}), bf16[3,5120,256]{2,1,0:T(8,128)(2,1)}) %all-gather.5.cloned.1.call-update) | async-done | bytes 7864336 | tf_op jit(solution)/shard_map/all_gather | solution.py:61
  167.7 9.0 %fusion.16 = bf16[3,512,256]{2,1,0:T(8,128)(2,1)S(1)} fusion(bf16[3,5120,256]{2,1,0:T(8,128)(2,1)} %all-gather.5.cloned.1.call-done, bf16[512,5120]{1,0:T(8,128)(2,1)} %all-gather.3.cloned.1.call-done), kind=kOutput, calls=%fused_computation.21 | convolution fusion | flops 4026925056 | bytes 13893632 | tf_op jit(solution)/shard_map/td,ide->ite/dot_general | solution.py:58
  176.7 2.1 %collective-permute-start = (bf16[2,256,256]{2,1,0:T(8,128)(2,1)S(1)}, bf16[2,256,256]{2,1,0:T(8,128)(2,1)S(1)}, u32[]{:S(2)}, u32[]{:S(2)}) collective-permute-start(bf16[2,256,256]{2,1,0:T(8,128)(2,1)S(1)} %get-tuple-element.7), channel_id=1, source_target_pairs={{0,4},{4,8},{8,12},{1,5},{5,9},{9,13},{2,6},{6,10},{10,14},{3,7},{... | collective-permute-start | bytes 786440 | tf_op jit(solution)/shard_map/ppermute | solution.py:19
  178.9 2.2 %collective-permute-start.1 = (bf16[2,256,256]{2,1,0:T(8,128)(2,1)S(1)}, bf16[2,256,256]{2,1,0:T(8,128)(2,1)S(1)}, u32[]{:S(2)}, u32[]{:S(2)}) collective-permute-start(bf16[2,256,256]{2,1,0:T(8,128)(2,1)S(1)} %get-tuple-element.8), channel_id=1, source_target_pairs={{4,0},{8,4},{12,8},{5,1},{9,5},{13,9},{6,2},{10,6},{14,10},{7,3},{... | collective-permute-start | bytes 786440 | tf_op jit(solution)/shard_map/ppermute | solution.py:20
  181.1 0.0 copy-done.4
  181.1 0.1 iota_compare_fusion
  181.3 0.1 reshape_squeeze.10
  181.3 0.8 collective-permute-done
  182.2 4.4 %collective-permute-done.1 = bf16[2,256,256]{2,1,0:T(8,128)(2,1)S(1)} collective-permute-done((bf16[2,256,256]{2,1,0:T(8,128)(2,1)S(1)}, bf16[2,256,256]{2,1,0:T(8,128)(2,1)S(1)}, u32[]{:S(2)}, u32[]{:S(2)}) %collective-permute-start.1) | collective-permute-done | bytes 262176 | tf_op jit(solution)/shard_map/ppermute | solution.py:20
  186.6 0.1 pad_maximum_fusion
  186.6 0.1 fusion.32
  186.7 0.1 reshape_squeeze.11
  186.9 0.1 copy.15
  187.0 0.8 gather_fusion.1
  187.8 0.1 copy.17
  187.9 0.5 fusion.28
  188.4 0.4 fusion.8
  188.8 0.6 fusion.9
  189.4 0.9 reshape_squeeze.9
  190.3 1.1 copy.14
  191.5 1.9 gather_fusion
  193.3 2.4 %fusion.25 = bf16[4,128,2,128]{1,3,2,0:T(8,128)(2,1)S(1)} fusion(f32[4,2,128,5,128]{2,4,3,1,0:T(8,128)S(1)} %bitcast.38, f32[4,2,128]{2,1,0:T(2,128)S(1)} %fusion.9, f32[4,2,128]{2,1,0:T(2,128)S(1)} %fusion.8, pred[4,5]{1,0:T(4,128)(4,1)S(1)} %iota_compare_fusion, bf16[4,5,128,2,128]{4,2,3,1,0:T(8,128)(2,1)} %bitcast.41), kind=kOutput, calls=%fused_computation.24 | convolution fusion | flops 171180032 | bytes 4202516 | tf_op jit(solution)/shard_map/phtks,pkshd->pthd/dot_general | solution.py:43
  195.8 0.2 copy.20
  195.9 0.7 copy.37
  (8 shorter events, 0.1 us)
Async XLA Ops:
  6.5 3.6 %copy-start = (bf16[128,5120]{1,0:T(8,128)(2,1)S(1)}, bf16[128,5120]{1,0:T(8,128)(2,1)}, u32[]{:S(2)}) copy-start(bf16[128,5120]{1,0:T(8,128)(2,1)} %param.6) | copy-start | bytes 3932164
  6.5 3.5 %copy-start.2 = (f32[5120]{0:T(1024)S(1)}, f32[5120]{0:T(1024)}, u32[]{:S(2)}) copy-start(f32[5120]{0:T(1024)} %param.8) | copy-start | bytes 61444
  6.5 3.6 %copy-start.1 = (f32[5120]{0:T(1024)S(1)}, f32[5120]{0:T(1024)}, u32[]{:S(2)}) copy-start(f32[5120]{0:T(1024)} %param.7) | copy-start | bytes 61444
  6.5 105.5 %all-gather.3.cloned.1.call-start = ((), (), s32[]{:S(2)}) async-start(), calls=%async_computation | async-start | bytes 6553600 | tf_op jit(solution)/shard_map/all_gather | solution.py:57
  10.1 2.4 %copy-start.3 = (s32[1,4,5]{2,1,0:T(4,128)S(1)}, s32[1,4,5]{2,1,0:T(4,128)}, u32[]{:S(2)}) copy-start(s32[1,4,5]{2,1,0:T(4,128)} %param.10) | copy-start | bytes 244
  11.8 155.9 %all-gather.5.cloned.1.call-start = ((), (), s32[]{:S(2)}) async-start(), calls=%async_computation.1 | async-start | bytes 9830400 | tf_op jit(solution)/shard_map/all_gather | solution.py:61
  12.7 168.5 %copy-start.4 = (s32[1,4]{1,0:T(1,128)S(1)}, s32[1,4]{1,0:T(1,128)}, u32[]{:S(2)}) copy-start(s32[1,4]{1,0:T(1,128)} %param.11) | copy-start | bytes 52
  176.7 5.4 %collective-permute-start = (bf16[2,256,256]{2,1,0:T(8,128)(2,1)S(1)}, bf16[2,256,256]{2,1,0:T(8,128)(2,1)S(1)}, u32[]{:S(2)}, u32[]{:S(2)}) collective-permute-start(bf16[2,256,256]{2,1,0:T(8,128)(2,1)S(1)} %get-tuple-element.7), channel_id=1, source_target_pairs={{0,4},{4,8},{8,12},{1,5},{5,9},{9,13},{2,6},{6,10},{10,14},{3,7},{... | collective-permute-start | bytes 786440 | tf_op jit(solution)/shard_map/ppermute | solution.py:19
  178.9 7.7 %collective-permute-start.1 = (bf16[2,256,256]{2,1,0:T(8,128)(2,1)S(1)}, bf16[2,256,256]{2,1,0:T(8,128)(2,1)S(1)}, u32[]{:S(2)}, u32[]{:S(2)}) collective-permute-start(bf16[2,256,256]{2,1,0:T(8,128)(2,1)S(1)} %get-tuple-element.8), channel_id=1, source_target_pairs={{4,0},{8,4},{12,8},{5,1},{9,5},{13,9},{6,2},{10,6},{14,10},{7,3},{... | collective-permute-start | bytes 786440 | tf_op jit(solution)/shard_map/ppermute | solution.py:20
Sparse Core Ops, SparseCore 0:
  11.9 100.1 all-gather.2
  113.6 54.0 all-gather.4
where the time goes:
time: 204 us
  waiting for transfers between devices  161 us (79%)
  between operations  13.6 us (7%)
  matrix products  11.9 us (6%)
  other arithmetic  6.35 us (3%)
  local copies, waits for them, and re-layouts  6.3 us (3%)
  starting transfers between devices  4.38 us (2%)
    all_gather x1, waiting for transfers between devices, shards(): gathered = lax.all_gather(normed, 'tensor', axis=0, tiled=True)  99.4 us
    all_gather x1, waiting for transfers between devices, shards(): lax.all_gather(w_qkv, 'block', axis=1, tiled=True)  55.6 us
    dot_general x1, matrix products, shards(): jnp.einsum('td,ide->ite', gathered, lax.all_gather(w_qkv, 'block', axis=1...  9.01 us
    ppermute x1, waiting for transfers between devices, with_halo(): after = lax.ppermute(first, axis, down)  4.4 us
  transfers between devices with their start and end apart: 4, of which 4 were waited for; matrix products, arithmetic and copies ran while one was open for 0% of the time, Pallas kernels for 0%

commit v1 on v0

--- a/solution.py
+++ b/solution.py
@@ -54,7 +54,14 @@
     normed = (centred * lax.rsqrt(row_var + epsilon) * (1.0 + mod_scale) + mod_shift).astype(
         jnp.bfloat16
     )
-    gathered = lax.all_gather(normed, "tensor", axis=0, tiled=True)
+    ring = [normed]
+    for hop in range(3):
+        ring.append(lax.ppermute(ring[-1], "tensor", [(dev, (dev + 1) % 4) for dev in range(4)]))
+    gathered = jnp.roll(
+        jnp.concatenate(ring[::-1], axis=0),
+        (lax.axis_index("tensor") + 1) * ring[0].shape[0],
+        axis=0,
+    )
     projected = jnp.einsum(
         "td,ide->ite",
         gathered,

time: 204 us -> 158 us (0.77)
  waiting for transfers between devices: 161 us -> 98 us
  local copies, waits for them, and re-layouts: 6.3 us -> 19.1 us
  starting transfers between devices: 4.38 us -> 9.62 us
    all_gather x1 -> x0, waiting for transfers between devices: 99.4 us -> none  [shards(): gathered = lax.all_gather(normed, 'tensor', axis=0, tiled=True)]
    ppermute x0 -> x3, waiting for transfers between devices: none -> 91.7 us  [shards(): lax.ppermute(ring[-1], 'tensor', [(dev, (dev + 1) % 4) for dev in range(4)])]
    all_gather x1, waiting for transfers between devices: 55.6 us -> 0.01 us  [shards(): lax.all_gather(w_qkv, 'block', axis=1, tiled=True)]
    unnamed x11 -> x17, local copies, waits for them, and re-layouts: 0.76 us -> 13.6 us
    ppermute x1, starting transfers between devices: 2.12 us -> 5.53 us  [with_halo(): before = lax.ppermute(last, axis, up)]
    ppermute x0 -> x3, starting transfers between devices: none -> 2.17 us  [shards(): lax.ppermute(ring[-1], 'tensor', [(dev, (dev + 1) % 4) for dev in range(4)])]
  transfers between devices with their start and end apart: 4 -> 6, of which waited for: 4 -> 5; matrix products, arithmetic and copies ran while one was open for 0% -> 11% of each run, Pallas kernels for 0% -> 0%
where the time goes in v1:
time: 158 us
  waiting for transfers between devices  98 us (62%)
  local copies, waits for them, and re-layouts  19.1 us (12%)
  between operations  13.6 us (9%)
  matrix products  11.9 us (8%)
  starting transfers between devices  9.62 us (6%)
  other arithmetic  5.78 us (4%)
    ppermute x3, waiting for transfers between devices, shards(): lax.ppermute(ring[-1], 'tensor', [(dev, (dev + 1) % 4) for dev in range(4)])  91.7 us
    unnamed x17, local copies, waits for them, and re-layouts  13.6 us
    dot_general x1, matrix products, shards(): jnp.einsum('td,ide->ite', gathered, lax.all_gather(w_qkv, 'block', axis=1...  9.02 us
    ppermute x1, starting transfers between devices, with_halo(): before = lax.ppermute(last, axis, up)  5.53 us
    ppermute x1, waiting for transfers between devices, with_halo(): after = lax.ppermute(first, axis, down)  4.4 us
  transfers between devices with their start and end apart: 6, of which 5 were waited for; matrix products, arithmetic and copies ran while one was open for 11% of the time, Pallas kernels for 0%

profile of v1, /device:TPU:1, one launch (start us, length us, event | category | flops | bytes accessed | tf_op | source)
XLA Modules:
  0.0 158.0 jit_solution(14880943317701691915)
XLA Ops:
  6.5 0.0 copy-start
  6.5 0.0 copy-start.2
  6.5 0.0 copy-start.1
  6.5 0.0 all-gather.2.cloned.1.call-start
  6.5 0.7 all-gather.2.cloned.1.call-update
  7.3 0.6 copy-done
  7.9 0.0 copy-start.3
  7.9 0.3 convert_reduce_fusion
  8.1 0.5 fusion.5
  8.6 0.0 copy-done.2
  8.7 0.0 copy-done.1
  8.7 0.6 fusion.8
  9.3 2.2 %collective-permute-start = (bf16[128,5120]{1,0:T(8,128)(2,1)S(1)}, bf16[128,5120]{1,0:T(8,128)(2,1)S(1)}, u32[]{:S(2)}, u32[]{:S(2)}) collective-permute-start(bf16[128,5120]{1,0:T(8,128)(2,1)S(1)} %fusion.8), channel_id=1, source_target_pairs={{0,1},{1,2},{2,3},{3,0},{4,5},{5,6},{6,7},{7,4},{8,9},{9,10},{10,1... | collective-permute-start | bytes 3932168 | tf_op jit(solution)/shard_map/ppermute | solution.py:59
  11.4 30.5 %collective-permute-done = bf16[128,5120]{1,0:T(8,128)(2,1)S(1)} collective-permute-done((bf16[128,5120]{1,0:T(8,128)(2,1)S(1)}, bf16[128,5120]{1,0:T(8,128)(2,1)S(1)}, u32[]{:S(2)}, u32[]{:S(2)}) %collective-permute-start) | collective-permute-done | bytes 1310752 | tf_op jit(solution)/shard_map/ppermute | solution.py:59
  41.9 0.0 collective-permute-start.1
  41.9 31.0 %collective-permute-done.1 = bf16[128,5120]{1,0:T(8,128)(2,1)} collective-permute-done((bf16[128,5120]{1,0:T(8,128)(2,1)S(1)}, bf16[128,5120]{1,0:T(8,128)(2,1)}, u32[]{:S(2)}, u32[]{:S(2)}) %collective-permute-start.1) | collective-permute-done | bytes 1310752 | tf_op jit(solution)/shard_map/ppermute | solution.py:59
  72.9 0.0 collective-permute-start.2
  72.9 0.0 copy-done.3
  72.9 0.1 reshape.73
  73.0 30.2 %collective-permute-done.2 = bf16[128,5120]{1,0:T(8,128)(2,1)} collective-permute-done((bf16[128,5120]{1,0:T(8,128)(2,1)}, bf16[128,5120]{1,0:T(8,128)(2,1)}, u32[]{:S(2)}, u32[]{:S(2)}) %collective-permute-start.2) | collective-permute-done | bytes 1310752 | tf_op jit(solution)/shard_map/ppermute | solution.py:59
  103.3 2.5 %constant_dynamic-update-slice_fusion.7 = bf16[1024,5120]{1,0:T(8,128)(2,1)} fusion(bf16[128,5120]{1,0:T(8,128)(2,1)} %collective-permute-done.2), kind=kLoop, calls=%fused_computation.37 | loop fusion | bytes 2621440
  105.7 2.5 %constant_dynamic-update-slice_fusion.6 = bf16[1024,5120]{1,0:T(8,128)(2,1)} fusion(bf16[1024,5120]{1,0:T(8,128)(2,1)} %constant_dynamic-update-slice_fusion.7, bf16[128,5120]{1,0:T(8,128)(2,1)} %collective-permute-done.1), kind=kLoop, calls=%fused_computation.36 | loop fusion | bytes 2621440
  108.2 1.2 constant_dynamic-update-slice_fusion.5
  109.3 1.6 %constant_dynamic-update-slice_fusion.4 = bf16[1024,5120]{1,0:T(8,128)(2,1)} fusion(bf16[1024,5120]{1,0:T(8,128)(2,1)} %constant_dynamic-update-slice_fusion.5, f32[5120]{0:T(1024)S(1)} %copy-done.1, f32[5120]{0:T(1024)S(1)} %broadcast_add_fusion, f32[128]{0:T(128)S(1)} %add_rsqrt_fusion, f32[128]{0:T(128)S(1)} %broadcast_multiply_fusion, ...), kind=kLoop, calls=%fused_computation.34 | loop fusion | flops 3932160 | bytes 2663424
  111.0 2.5 %constant_dynamic-update-slice_fusion.3 = bf16[1024,5120]{1,0:T(8,128)(2,1)} fusion(bf16[1024,5120]{1,0:T(8,128)(2,1)} %constant_dynamic-update-slice_fusion.4, bf16[128,5120]{1,0:T(8,128)(2,1)} %collective-permute-done.2), kind=kLoop, calls=%fused_computation.33 | loop fusion | bytes 2621440
  113.5 2.5 %constant_dynamic-update-slice_fusion.2 = bf16[1024,5120]{1,0:T(8,128)(2,1)} fusion(bf16[1024,5120]{1,0:T(8,128)(2,1)} %constant_dynamic-update-slice_fusion.3, bf16[128,5120]{1,0:T(8,128)(2,1)} %collective-permute-done.1), kind=kLoop, calls=%fused_computation.32 | loop fusion | bytes 2621440
  115.9 1.2 constant_dynamic-update-slice_fusion.1
  117.2 1.6 %constant_dynamic-update-slice_fusion = bf16[1024,5120]{1,0:T(8,128)(2,1)} fusion(bf16[1024,5120]{1,0:T(8,128)(2,1)} %constant_dynamic-update-slice_fusion.1, f32[5120]{0:T(1024)S(1)} %copy-done.1, f32[5120]{0:T(1024)S(1)} %broadcast_add_fusion, f32[128]{0:T(128)S(1)} %add_rsqrt_fusion, f32[128]{0:T(128)S(1)} %broadcast_multiply_fusion, ...), kind=kLoop, calls=%fused_computation.30 | loop fusion | flops 3932160 | bytes 2663424 | tf_op jit(solution)/shard_map/jit(_roll_dynamic)/concatenate | solution.py:60
  118.8 0.0 copy-start.4
  118.8 0.0 all-gather.2.cloned.1.call-done
  118.8 9.0 %fusion.17 = bf16[3,512,256]{2,1,0:T(8,128)(2,1)S(1)} fusion(bf16[3,5120,256]{2,1,0:T(8,128)(2,1)} %all-gather.2.cloned.1.call-done, bf16[1024,5120]{1,0:T(8,128)(2,1)} %constant_dynamic-update-slice_fusion, s32[]{:T(128)S(6)} %select_n.29), kind=kOutput, calls=%fused_computation.22 | convolution fusion | flops 4026925056 | bytes 13893636 | tf_op jit(solution)/shard_map/td,ide->ite/dot_general | solution.py:65
  127.9 5.5 %collective-permute-start.3 = (bf16[2,256,256]{2,1,0:T(8,128)(2,1)S(1)}, bf16[2,256,256]{2,1,0:T(8,128)(2,1)S(1)}, u32[]{:S(2)}, u32[]{:S(2)}) collective-permute-start(bf16[2,256,256]{2,1,0:T(8,128)(2,1)S(1)} %get-tuple-element.7), channel_id=1, source_target_pairs={{0,4},{4,8},{8,12},{1,5},{5,9},{9,13},{2,6},{6,10},{10,14},{3,7},{... | collective-permute-start | bytes 786440 | tf_op jit(solution)/shard_map/ppermute | solution.py:19
  133.4 1.9 %collective-permute-start.4 = (bf16[2,256,256]{2,1,0:T(8,128)(2,1)S(1)}, bf16[2,256,256]{2,1,0:T(8,128)(2,1)S(1)}, u32[]{:S(2)}, u32[]{:S(2)}) collective-permute-start(bf16[2,256,256]{2,1,0:T(8,128)(2,1)S(1)} %get-tuple-element.8), channel_id=1, source_target_pairs={{4,0},{8,4},{12,8},{5,1},{9,5},{13,9},{6,2},{10,6},{14,10},{7,3},{... | collective-permute-start | bytes 786440 | tf_op jit(solution)/shard_map/ppermute | solution.py:20
  135.4 0.0 copy-done.4
  135.4 0.1 iota_compare_fusion
  135.5 0.1 reshape_squeeze.10
  135.6 1.1 collective-permute-done.3
  136.7 4.4 %collective-permute-done.4 = bf16[2,256,256]{2,1,0:T(8,128)(2,1)S(1)} collective-permute-done((bf16[2,256,256]{2,1,0:T(8,128)(2,1)S(1)}, bf16[2,256,256]{2,1,0:T(8,128)(2,1)S(1)}, u32[]{:S(2)}, u32[]{:S(2)}) %collective-permute-start.4) | collective-permute-done | bytes 262176 | tf_op jit(solution)/shard_map/ppermute | solution.py:20
  141.1 0.1 pad_maximum_fusion
  141.2 0.1 fusion.34
  141.3 0.1 reshape_squeeze.11
  141.4 0.1 copy.15
  141.5 0.8 gather_fusion.1
  142.3 0.1 copy.17
  142.4 0.5 fusion.29
  142.9 0.4 fusion.9
  143.3 0.6 fusion.10
  143.9 0.9 reshape_squeeze.9
  144.8 1.1 copy.14
  146.0 1.9 %gather_fusion = bf16[20,128,2,128]{3,1,2,0:T(8,128)(2,1)} fusion(bf16[8,128,2,128]{3,1,2,0:T(8,128)(2,1)S(1)} %copy.14, s32[1024]{0:T(1024)S(1)} %pad_clamp_fusion), kind=kCustom, calls=%fused_computation | custom fusion | bytes 2621520 | tf_op jit(solution)/shard_map/gather | solution.py:32
  147.8 2.4 %fusion.26 = bf16[4,128,2,128]{1,3,2,0:T(8,128)(2,1)S(1)} fusion(f32[4,2,128,5,128]{2,4,3,1,0:T(8,128)S(1)} %bitcast.38, f32[4,2,128]{2,1,0:T(2,128)S(1)} %fusion.10, f32[4,2,128]{2,1,0:T(2,128)S(1)} %fusion.9, pred[4,5]{1,0:T(4,128)(4,1)S(1)} %iota_compare_fusion, bf16[4,5,128,2,128]{4,2,3,1,0:T(8,128)(2,1)} %bitcast.41), kind=kOutput, calls=%fused_computation.25 | convolution fusion | flops 171180032 | bytes 4202516 | tf_op jit(solution)/shard_map/phtks,pkshd->pthd/dot_general | solution.py:43
  150.2 0.2 copy.20
  150.4 0.7 copy.37
  (8 shorter events, 0.1 us)
Async XLA Ops:
  6.5 1.3 copy-start
  6.5 2.1 %copy-start.2 = (f32[5120]{0:T(1024)S(1)}, f32[5120]{0:T(1024)}, u32[]{:S(2)}) copy-start(f32[5120]{0:T(1024)} %param.8) | copy-start | bytes 61444
  6.5 2.1 %copy-start.1 = (f32[5120]{0:T(1024)S(1)}, f32[5120]{0:T(1024)}, u32[]{:S(2)}) copy-start(f32[5120]{0:T(1024)} %param.7) | copy-start | bytes 61444
  6.5 112.3 %all-gather.2.cloned.1.call-start = ((), (), s32[]{:S(2)}) async-start(), calls=%async_computation | async-start | bytes 9830400 | tf_op jit(solution)/shard_map/all_gather | solution.py:68
  7.9 65.1 %copy-start.3 = (s32[1,4,5]{2,1,0:T(4,128)S(1)}, s32[1,4,5]{2,1,0:T(4,128)}, u32[]{:S(2)}) copy-start(s32[1,4,5]{2,1,0:T(4,128)} %param.10) | copy-start | bytes 244
  9.3 32.7 %collective-permute-start = (bf16[128,5120]{1,0:T(8,128)(2,1)S(1)}, bf16[128,5120]{1,0:T(8,128)(2,1)S(1)}, u32[]{:S(2)}, u32[]{:S(2)}) collective-permute-start(bf16[128,5120]{1,0:T(8,128)(2,1)S(1)} %fusion.8), channel_id=1, source_target_pairs={{0,1},{1,2},{2,3},{3,0},{4,5},{5,6},{6,7},{7,4},{8,9},{9,10},{10,1... | collective-permute-start | bytes 3932168 | tf_op jit(solution)/shard_map/ppermute | solution.py:59
  41.9 31.0 %collective-permute-start.1 = (bf16[128,5120]{1,0:T(8,128)(2,1)S(1)}, bf16[128,5120]{1,0:T(8,128)(2,1)}, u32[]{:S(2)}, u32[]{:S(2)}) collective-permute-start(bf16[128,5120]{1,0:T(8,128)(2,1)S(1)} %collective-permute-done), channel_id=1, source_target_pairs={{0,1},{1,2},{2,3},{3,0},{4,5},{5,6},{6,7},{7,4},{8,9},{9,10},{10,1... | collective-permute-start | bytes 3932168 | tf_op jit(solution)/shard_map/ppermute | solution.py:59
  72.9 30.3 %collective-permute-start.2 = (bf16[128,5120]{1,0:T(8,128)(2,1)}, bf16[128,5120]{1,0:T(8,128)(2,1)}, u32[]{:S(2)}, u32[]{:S(2)}) collective-permute-start(bf16[128,5120]{1,0:T(8,128)(2,1)} %collective-permute-done.1), channel_id=1, source_target_pairs={{0,1},{1,2},{2,3},{3,0},{4,5},{5,6},{6,7},{7,4},{8,9},{9,10},{10,1... | collective-permute-start | bytes 3932168 | tf_op jit(solution)/shard_map/ppermute | solution.py:59
  118.8 16.6 %copy-start.4 = (s32[1,4]{1,0:T(1,128)S(1)}, s32[1,4]{1,0:T(1,128)}, u32[]{:S(2)}) copy-start(s32[1,4]{1,0:T(1,128)} %param.11) | copy-start | bytes 52
  127.9 8.8 %collective-permute-start.3 = (bf16[2,256,256]{2,1,0:T(8,128)(2,1)S(1)}, bf16[2,256,256]{2,1,0:T(8,128)(2,1)S(1)}, u32[]{:S(2)}, u32[]{:S(2)}) collective-permute-start(bf16[2,256,256]{2,1,0:T(8,128)(2,1)S(1)} %get-tuple-element.7), channel_id=1, source_target_pairs={{0,4},{4,8},{8,12},{1,5},{5,9},{9,13},{2,6},{6,10},{10,14},{3,7},{... | collective-permute-start | bytes 786440 | tf_op jit(solution)/shard_map/ppermute | solution.py:19
  133.4 7.7 %collective-permute-start.4 = (bf16[2,256,256]{2,1,0:T(8,128)(2,1)S(1)}, bf16[2,256,256]{2,1,0:T(8,128)(2,1)S(1)}, u32[]{:S(2)}, u32[]{:S(2)}) collective-permute-start(bf16[2,256,256]{2,1,0:T(8,128)(2,1)S(1)} %get-tuple-element.8), channel_id=1, source_target_pairs={{4,0},{8,4},{12,8},{5,1},{9,5},{13,9},{6,2},{10,6},{14,10},{7,3},{... | collective-permute-start | bytes 786440 | tf_op jit(solution)/shard_map/ppermute | solution.py:20
Sparse Core Ops, SparseCore 0:
  8.9 57.7 all-gather.1
